TPU v7x, 256 devices: a whole 4x4x8 slice. The times are simulated.
256 devices in a mesh: row: 8 (over y, x_lo), col: 32 (over z, x_hi, core).
Axes of the slice: x: 4 (x_hi: 2, x_lo: 2; x = x_hi * 2 + x_lo), y: 4, z: 8, core: 2. Of those that a mesh axis runs over, the one named last changes fastest.
Arguments:
- tile_values: bfloat16 [8192, 8192], P('row', 'col'), may hold values from -1.5 to 1.5
- upper_mask: int32 [128, 128], P('row', 'col'), may hold values from 0 to 1, as said below
Outputs:
- layer_partials: float32 [8192, 32768], P('row', 'col')
Inputs may be any that keep to these rules, and one draw needn't show every extreme that they name: `upper_mask`: every diagonal tile is set.
All inputs are finite; a program needn't handle non-finite values.
Results may differ from a plain program's by a relative error of at most 0.00059.
Values may be sent and summed in bfloat16 or wider, within the bound.
A program may use at most 128 MiB of HBM per device.

v0:
```python
from functools import partial

import jax
import jax.numpy as jnp
from jax import lax
from jax.sharding import PartitionSpec as P

TILE = 64


def swapped(value, axis, apart):
    mask = 2**apart
    pairs = [(source, source ^ mask) for source in range(lax.axis_size(axis))]
    return lax.ppermute(value, axis, pairs)


def from_behind(value, axis, steps):
    count = lax.axis_size(axis)
    pairs = [(source, (source + steps) % count) for source in range(count)]
    return lax.ppermute(value, axis, pairs)


def bit_count(amount):
    return amount.bit_length() - 1


def xor_order(slot_grid, slot_bits, owner_index):
    result = slot_grid
    for bit_level in range(slot_bits):
        flipped = jnp.flip(result, slot_bits - 1 - bit_level)
        chosen = owner_index >> bit_level & 1 == 1
        result = jnp.where(chosen, flipped, result)
    return result


def grid_transpose(field_data, row_bits, group_bits, col_bits, row_index, block_col):
    for bit_level in range(row_bits):
        turned = field_data
        for bit_place in (group_bits + bit_level, col_bits + bit_level):
            turned = swapped(turned, ("row", "col"), bit_place)
        differ = row_index >> bit_level & 1 != block_col >> bit_level & 1
        field_data = jnp.where(differ, turned, field_data)
    return field_data


def shift_left(field_data, count, groups):
    return from_behind(field_data, "col", -count * groups)


def shift_right(field_data, count):
    return from_behind(field_data, "row", -count)


def skew_by(field_data, mover, amount_index, row_bits):
    for bit_level in range(row_bits):
        moved_field = mover(field_data, 1 << bit_level)
        chosen = amount_index >> bit_level & 1 == 1
        field_data = jnp.where(chosen, moved_field, field_data)
    return field_data


def window_product(left_now, right_now):
    return jnp.dot(left_now, right_now, preferred_element_type=jnp.float32)


def shards(tile_values, upper_mask):
    rows_total = lax.axis_size("row")
    cols_total = lax.axis_size("col")
    groups = cols_total // rows_total
    group_bits = bit_count(groups)
    row_bits = bit_count(rows_total)
    col_bits = bit_count(cols_total)
    row_index = lax.axis_index("row")
    col_index = lax.axis_index("col")
    layer_index = col_index % groups
    block_col = col_index // groups
    height = tile_values.shape[0]
    piece_width = tile_values.shape[1]
    tiles_high = height // TILE
    tiles_wide = piece_width // TILE
    tile_rows = row_index * tiles_high + jnp.arange(tiles_high, dtype=jnp.int32)
    tile_cols = col_index * tiles_wide + jnp.arange(tiles_wide, dtype=jnp.int32)
    keep_tiles = (upper_mask != 0) & (tile_rows[:, None] <= tile_cols[None, :])
    keep_cells = jnp.repeat(jnp.repeat(keep_tiles, TILE, axis=0), TILE, axis=1)
    upper_piece = jnp.where(keep_cells, tile_values, jnp.zeros_like(tile_values))
    slot_shape = (2,) * group_bits + (piece_width, piece_width)
    slot_grid = xor_order(upper_piece.reshape(slot_shape), group_bits, layer_index)
    for bit_level in range(group_bits):
        axis_place = group_bits - 1 - bit_level
        staying = lax.index_in_dim(slot_grid, 0, axis_place, keepdims=False)
        moving = lax.index_in_dim(slot_grid, 1, axis_place, keepdims=False)
        arrived = swapped(moving, "col", bit_level)
        slot_grid = jnp.stack([staying, arrived], axis_place)
    ordered = xor_order(slot_grid, group_bits, layer_index).reshape(
        groups, piece_width, piece_width
    )
    rows_turned = jnp.swapaxes(ordered, 1, 2).reshape(height, piece_width)
    move_left = partial(shift_left, groups=groups)
    mirrored = grid_transpose(rows_turned, row_bits, group_bits, col_bits, row_index, block_col)
    left_piece = (upper_piece.astype(jnp.float32) + mirrored.astype(jnp.float32)).astype(
        jnp.bfloat16
    )
    left_now = skew_by(left_piece, move_left, row_index, row_bits)
    right_now = grid_transpose(left_now, row_bits, group_bits, col_bits, row_index, block_col).T
    window_sum = window_product(left_now, right_now)
    left_now = move_left(left_now, 1)
    right_now = shift_right(right_now, 1)
    window_sum = window_sum + window_product(left_now, right_now)
    return window_sum


def solution(mesh):
    in_specs = (P("row", "col"), P("row", "col"))
    out_specs = P("row", "col")
    return jax.shard_map(shards, mesh=mesh, in_specs=in_specs, out_specs=out_specs, check_vma=False)
```

profile of v0, /device:TPU:23, one launch (start us, length us, event | category | flops | bytes accessed | tf_op | source)
XLA Modules:
  0.0 310.2 jit_solution(5936652984451551304)
XLA Ops:
  6.6 7.9 %collective-permute-done.1 = bf16[2,256,256]{2,1,0:T(8,128)(2,1)S(1)} collective-permute-done((bf16[2,256,256]{2,1,0:T(8,128)(2,1)S(1)}, bf16[2,256,256]{2,1,0:T(8,128)(2,1)S(1)}, u32[]{:S(2)}, u32[]{:S(2)}) %collective-permute-start.1) | collective-permute-done | bytes 262176 | tf_op jit(solution)/shard_map/ppermute | solution.py:14
  16.6 10.9 %collective-permute-done.2 = bf16[1024,256]{0,1:T(8,128)(2,1)S(1)} collective-permute-done((bf16[1024,256]{0,1:T(8,128)(2,1)S(1)}, bf16[1024,256]{0,1:T(8,128)(2,1)S(1)}, u32[]{:S(2)}, u32[]{:S(2)}) %collective-permute-start.2) | collective-permute-done | bytes 524320 | tf_op jit(solution)/shard_map/ppermute | solution.py:14
  28.1 10.9 %collective-permute-done.3 = bf16[1024,256]{0,1:T(8,128)(2,1)S(1)} collective-permute-done((bf16[1024,256]{0,1:T(8,128)(2,1)S(1)}, bf16[1024,256]{0,1:T(8,128)(2,1)S(1)}, u32[]{:S(2)}, u32[]{:S(2)}) %collective-permute-start.3) | collective-permute-done | bytes 524320 | tf_op jit(solution)/shard_map/ppermute | solution.py:14
  39.1 3.1 collective-permute-start.4
  42.2 22.7 %collective-permute-done.4 = bf16[1024,256]{0,1:T(8,128)(2,1)S(1)} collective-permute-done((bf16[1024,256]{0,1:T(8,128)(2,1)S(1)}, bf16[1024,256]{0,1:T(8,128)(2,1)S(1)}, u32[]{:S(2)}, u32[]{:S(2)}) %collective-permute-start.4) | collective-permute-done | bytes 524320 | tf_op jit(solution)/shard_map/ppermute | solution.py:14
  65.9 11.0 %collective-permute-done.5 = bf16[1024,256]{0,1:T(8,128)(2,1)S(1)} collective-permute-done((bf16[1024,256]{0,1:T(8,128)(2,1)S(1)}, bf16[1024,256]{0,1:T(8,128)(2,1)S(1)}, u32[]{:S(2)}, u32[]{:S(2)}) %collective-permute-start.5) | collective-permute-done | bytes 524320 | tf_op jit(solution)/shard_map/ppermute | solution.py:14
  77.0 6.6 %collective-permute-start.6 = (bf16[1024,256]{0,1:T(8,128)(2,1)S(1)}, bf16[1024,256]{0,1:T(8,128)(2,1)S(1)}, u32[]{:S(2)}, u32[]{:S(2)}) collective-permute-start(bf16[1024,256]{0,1:T(8,128)(2,1)S(1)} %broadcast_select_fusion.3), channel_id=1, source_target_pairs={{0,16},{1,17},{2,18},{3,19},{4,20},{5,21},{6,22},{7,23},{8,24},{9,... | collective-permute-start | bytes 1572872 | tf_op jit(solution)/shard_map/ppermute | solution.py:14
  83.6 19.4 %collective-permute-done.6 = bf16[1024,256]{0,1:T(8,128)(2,1)S(1)} collective-permute-done((bf16[1024,256]{0,1:T(8,128)(2,1)S(1)}, bf16[1024,256]{0,1:T(8,128)(2,1)S(1)}, u32[]{:S(2)}, u32[]{:S(2)}) %collective-permute-start.6) | collective-permute-done | bytes 524320 | tf_op jit(solution)/shard_map/ppermute | solution.py:14
  103.1 10.0 %collective-permute-done.7 = bf16[1024,256]{0,1:T(8,128)(2,1)S(1)} collective-permute-done((bf16[1024,256]{0,1:T(8,128)(2,1)S(1)}, bf16[1024,256]{0,1:T(8,128)(2,1)S(1)}, u32[]{:S(2)}, u32[]{:S(2)}) %collective-permute-start.7) | collective-permute-done | bytes 524320 | tf_op jit(solution)/shard_map/ppermute | solution.py:14
  113.4 11.4 %collective-permute-start.8 = (bf16[1024,256]{0,1:T(8,128)(2,1)S(1)}, bf16[1024,256]{0,1:T(8,128)(2,1)S(1)}, u32[]{:S(2)}, u32[]{:S(2)}) collective-permute-start(bf16[1024,256]{0,1:T(8,128)(2,1)S(1)} %add_convert_fusion), channel_id=1, source_target_pairs={{0,28},{1,29},{2,30},{3,31},{4,0},{5,1},{6,2},{7,3},{8,4},{9,5},{1... | collective-permute-start | bytes 1572872 | tf_op jit(solution)/shard_map/ppermute | solution.py:20
  124.7 9.7 %collective-permute-done.8 = bf16[1024,256]{0,1:T(8,128)(2,1)S(1)} collective-permute-done((bf16[1024,256]{0,1:T(8,128)(2,1)S(1)}, bf16[1024,256]{0,1:T(8,128)(2,1)S(1)}, u32[]{:S(2)}, u32[]{:S(2)}) %collective-permute-start.8) | collective-permute-done | bytes 524320 | tf_op jit(solution)/shard_map/ppermute | solution.py:20
  136.7 13.1 %collective-permute-done.9 = bf16[1024,256]{0,1:T(8,128)(2,1)S(1)} collective-permute-done((bf16[1024,256]{0,1:T(8,128)(2,1)S(1)}, bf16[1024,256]{0,1:T(8,128)(2,1)S(1)}, u32[]{:S(2)}, u32[]{:S(2)}) %collective-permute-start.9) | collective-permute-done | bytes 524320 | tf_op jit(solution)/shard_map/ppermute | solution.py:20
  149.9 4.3 %collective-permute-start.10 = (bf16[1024,256]{0,1:T(8,128)(2,1)S(1)}, bf16[1024,256]{0,1:T(8,128)(2,1)S(1)}, u32[]{:S(2)}, u32[]{:S(2)}) collective-permute-start(bf16[1024,256]{0,1:T(8,128)(2,1)S(1)} %broadcast_select_fusion.6), channel_id=1, source_target_pairs={{0,16},{1,17},{2,18},{3,19},{4,20},{5,21},{6,22},{7,23},{8,24},{9,... | collective-permute-start | bytes 1572872 | tf_op jit(solution)/shard_map/ppermute | solution.py:20
  154.3 14.4 %collective-permute-done.10 = bf16[1024,256]{0,1:T(8,128)(2,1)S(1)} collective-permute-done((bf16[1024,256]{0,1:T(8,128)(2,1)S(1)}, bf16[1024,256]{0,1:T(8,128)(2,1)S(1)}, u32[]{:S(2)}, u32[]{:S(2)}) %collective-permute-start.10) | collective-permute-done | bytes 524320 | tf_op jit(solution)/shard_map/ppermute | solution.py:20
  168.7 11.6 %collective-permute-start.11 = (bf16[1024,256]{0,1:T(8,128)(2,1)S(1)}, bf16[1024,256]{0,1:T(8,128)(2,1)S(1)}, u32[]{:S(2)}, u32[]{:S(2)}) collective-permute-start(bf16[1024,256]{0,1:T(8,128)(2,1)S(1)} %broadcast_select_fusion.7), channel_id=1, source_target_pairs={{0,4},{1,5},{2,6},{3,7},{4,0},{5,1},{6,2},{7,3},{8,12},{9,13},{10,... | collective-permute-start | bytes 1572872 | tf_op jit(solution)/shard_map/ppermute | solution.py:14
  180.3 18.4 %collective-permute-done.11 = bf16[1024,256]{0,1:T(8,128)(2,1)S(1)} collective-permute-done((bf16[1024,256]{0,1:T(8,128)(2,1)S(1)}, bf16[1024,256]{0,1:T(8,128)(2,1)S(1)}, u32[]{:S(2)}, u32[]{:S(2)}) %collective-permute-start.11) | collective-permute-done | bytes 524320 | tf_op jit(solution)/shard_map/ppermute | solution.py:14
  199.2 11.4 %collective-permute-done.12 = bf16[1024,256]{0,1:T(8,128)(2,1)S(1)} collective-permute-done((bf16[1024,256]{0,1:T(8,128)(2,1)S(1)}, bf16[1024,256]{0,1:T(8,128)(2,1)S(1)}, u32[]{:S(2)}, u32[]{:S(2)}) %collective-permute-start.12) | collective-permute-done | bytes 524320 | tf_op jit(solution)/shard_map/ppermute | solution.py:14
  210.7 4.5 %collective-permute-start.13 = (bf16[1024,256]{0,1:T(8,128)(2,1)S(1)}, bf16[1024,256]{0,1:T(8,128)(2,1)S(1)}, u32[]{:S(2)}, u32[]{:S(2)}) collective-permute-start(bf16[1024,256]{0,1:T(8,128)(2,1)S(1)} %broadcast_select_fusion), channel_id=1, source_target_pairs={{0,8},{1,9},{2,10},{3,11},{4,12},{5,13},{6,14},{7,15},{8,0},{9,1},... | collective-permute-start | bytes 1572872 | tf_op jit(solution)/shard_map/ppermute | solution.py:14
  215.2 23.0 %collective-permute-done.13 = bf16[1024,256]{0,1:T(8,128)(2,1)S(1)} collective-permute-done((bf16[1024,256]{0,1:T(8,128)(2,1)S(1)}, bf16[1024,256]{0,1:T(8,128)(2,1)S(1)}, u32[]{:S(2)}, u32[]{:S(2)}) %collective-permute-start.13) | collective-permute-done | bytes 524320 | tf_op jit(solution)/shard_map/ppermute | solution.py:14
  239.2 11.3 %collective-permute-done.14 = bf16[1024,256]{0,1:T(8,128)(2,1)S(1)} collective-permute-done((bf16[1024,256]{0,1:T(8,128)(2,1)S(1)}, bf16[1024,256]{0,1:T(8,128)(2,1)S(1)}, u32[]{:S(2)}, u32[]{:S(2)}) %collective-permute-start.14) | collective-permute-done | bytes 524320 | tf_op jit(solution)/shard_map/ppermute | solution.py:14
  250.5 3.3 %collective-permute-start.15 = (bf16[1024,256]{0,1:T(8,128)(2,1)S(1)}, bf16[1024,256]{0,1:T(8,128)(2,1)S(1)}, u32[]{:S(2)}, u32[]{:S(2)}) collective-permute-start(bf16[1024,256]{0,1:T(8,128)(2,1)S(1)} %broadcast_select_fusion.2), channel_id=1, source_target_pairs={{0,16},{1,17},{2,18},{3,19},{4,20},{5,21},{6,22},{7,23},{8,24},{9,... | collective-permute-start | bytes 1572872 | tf_op jit(solution)/shard_map/ppermute | solution.py:14
  253.8 25.6 %collective-permute-done.15 = bf16[1024,256]{0,1:T(8,128)(2,1)S(1)} collective-permute-done((bf16[1024,256]{0,1:T(8,128)(2,1)S(1)}, bf16[1024,256]{0,1:T(8,128)(2,1)S(1)}, u32[]{:S(2)}, u32[]{:S(2)}) %collective-permute-start.15) | collective-permute-done | bytes 524320 | tf_op jit(solution)/shard_map/ppermute | solution.py:14
  279.5 14.3 %collective-permute-done.16 = bf16[1024,256]{0,1:T(8,128)(2,1)S(1)} collective-permute-done((bf16[1024,256]{0,1:T(8,128)(2,1)S(1)}, bf16[1024,256]{0,1:T(8,128)(2,1)S(1)}, u32[]{:S(2)}, u32[]{:S(2)}) %collective-permute-start.16) | collective-permute-done | bytes 524320 | tf_op jit(solution)/shard_map/ppermute | solution.py:14
  294.4 12.2 %collective-permute-done.18 = bf16[256,1024]{1,0:T(8,128)(2,1)S(1)} collective-permute-done((bf16[256,1024]{1,0:T(8,128)(2,1)S(1)}, bf16[256,1024]{1,0:T(8,128)(2,1)S(1)}, u32[]{:S(2)}, u32[]{:S(2)}) %collective-permute-start.18) | collective-permute-done | bytes 524320 | tf_op jit(solution)/shard_map/ppermute | solution.py:20
  (43 shorter events, 19.0 us)
Async XLA Ops:
  3.4 1.9 collective-permute-start
  5.4 9.1 %collective-permute-start.1 = (bf16[2,256,256]{2,1,0:T(8,128)(2,1)S(1)}, bf16[2,256,256]{2,1,0:T(8,128)(2,1)S(1)}, u32[]{:S(2)}, u32[]{:S(2)}) collective-permute-start(bf16[2,256,256]{2,1,0:T(8,128)(2,1)S(1)} %get-tuple-element.6), channel_id=1, source_target_pairs={{0,2},{1,3},{2,0},{3,1},{4,6},{5,7},{6,4},{7,5},{8,10},{9,11},{10,... | collective-permute-start | bytes 786440 | tf_op jit(solution)/shard_map/ppermute | solution.py:14
  14.9 12.7 %collective-permute-start.2 = (bf16[1024,256]{0,1:T(8,128)(2,1)S(1)}, bf16[1024,256]{0,1:T(8,128)(2,1)S(1)}, u32[]{:S(2)}, u32[]{:S(2)}) collective-permute-start(bf16[1024,256]{0,1:T(8,128)(2,1)S(1)} %bitcast.22), channel_id=1, source_target_pairs={{0,4},{1,5},{2,6},{3,7},{4,0},{5,1},{6,2},{7,3},{8,12},{9,13},{10,... | collective-permute-start | bytes 1572872 | tf_op jit(solution)/shard_map/ppermute | solution.py:14
  27.6 11.5 %collective-permute-start.3 = (bf16[1024,256]{0,1:T(8,128)(2,1)S(1)}, bf16[1024,256]{0,1:T(8,128)(2,1)S(1)}, u32[]{:S(2)}, u32[]{:S(2)}) collective-permute-start(bf16[1024,256]{0,1:T(8,128)(2,1)S(1)} %collective-permute-done.2), channel_id=1, source_target_pairs={{0,32},{1,33},{2,34},{3,35},{4,36},{5,37},{6,38},{7,39},{8,40},{9,... | collective-permute-start | bytes 1572872 | tf_op jit(solution)/shard_map/ppermute | solution.py:14
  39.1 25.8 %collective-permute-start.4 = (bf16[1024,256]{0,1:T(8,128)(2,1)S(1)}, bf16[1024,256]{0,1:T(8,128)(2,1)S(1)}, u32[]{:S(2)}, u32[]{:S(2)}) collective-permute-start(bf16[1024,256]{0,1:T(8,128)(2,1)S(1)} %broadcast_select_fusion.1), channel_id=1, source_target_pairs={{0,8},{1,9},{2,10},{3,11},{4,12},{5,13},{6,14},{7,15},{8,0},{9,1},... | collective-permute-start | bytes 1572872 | tf_op jit(solution)/shard_map/ppermute | solution.py:14
  64.9 12.0 %collective-permute-start.5 = (bf16[1024,256]{0,1:T(8,128)(2,1)S(1)}, bf16[1024,256]{0,1:T(8,128)(2,1)S(1)}, u32[]{:S(2)}, u32[]{:S(2)}) collective-permute-start(bf16[1024,256]{0,1:T(8,128)(2,1)S(1)} %collective-permute-done.4), channel_id=1, source_target_pairs={{0,64},{1,65},{2,66},{3,67},{4,68},{5,69},{6,70},{7,71},{8,72},{9,... | collective-permute-start | bytes 1572872 | tf_op jit(solution)/shard_map/ppermute | solution.py:14
  77.0 26.0 %collective-permute-start.6 = (bf16[1024,256]{0,1:T(8,128)(2,1)S(1)}, bf16[1024,256]{0,1:T(8,128)(2,1)S(1)}, u32[]{:S(2)}, u32[]{:S(2)}) collective-permute-start(bf16[1024,256]{0,1:T(8,128)(2,1)S(1)} %broadcast_select_fusion.3), channel_id=1, source_target_pairs={{0,16},{1,17},{2,18},{3,19},{4,20},{5,21},{6,22},{7,23},{8,24},{9,... | collective-permute-start | bytes 1572872 | tf_op jit(solution)/shard_map/ppermute | solution.py:14
  103.0 10.1 %collective-permute-start.7 = (bf16[1024,256]{0,1:T(8,128)(2,1)S(1)}, bf16[1024,256]{0,1:T(8,128)(2,1)S(1)}, u32[]{:S(2)}, u32[]{:S(2)}) collective-permute-start(bf16[1024,256]{0,1:T(8,128)(2,1)S(1)} %collective-permute-done.6), channel_id=1, source_target_pairs={{0,128},{1,129},{2,130},{3,131},{4,132},{5,133},{6,134},{7,135},{8... | collective-permute-start | bytes 1572872 | tf_op jit(solution)/shard_map/ppermute | solution.py:14
  113.4 21.0 %collective-permute-start.8 = (bf16[1024,256]{0,1:T(8,128)(2,1)S(1)}, bf16[1024,256]{0,1:T(8,128)(2,1)S(1)}, u32[]{:S(2)}, u32[]{:S(2)}) collective-permute-start(bf16[1024,256]{0,1:T(8,128)(2,1)S(1)} %add_convert_fusion), channel_id=1, source_target_pairs={{0,28},{1,29},{2,30},{3,31},{4,0},{5,1},{6,2},{7,3},{8,4},{9,5},{1... | collective-permute-start | bytes 1572872 | tf_op jit(solution)/shard_map/ppermute | solution.py:20
  134.5 15.4 %collective-permute-start.9 = (bf16[1024,256]{0,1:T(8,128)(2,1)S(1)}, bf16[1024,256]{0,1:T(8,128)(2,1)S(1)}, u32[]{:S(2)}, u32[]{:S(2)}) collective-permute-start(bf16[1024,256]{0,1:T(8,128)(2,1)S(1)} %broadcast_select_fusion.5), channel_id=1, source_target_pairs={{0,24},{1,25},{2,26},{3,27},{4,28},{5,29},{6,30},{7,31},{8,0},{9,1... | collective-permute-start | bytes 1572872 | tf_op jit(solution)/shard_map/ppermute | solution.py:20
  149.9 18.7 %collective-permute-start.10 = (bf16[1024,256]{0,1:T(8,128)(2,1)S(1)}, bf16[1024,256]{0,1:T(8,128)(2,1)S(1)}, u32[]{:S(2)}, u32[]{:S(2)}) collective-permute-start(bf16[1024,256]{0,1:T(8,128)(2,1)S(1)} %broadcast_select_fusion.6), channel_id=1, source_target_pairs={{0,16},{1,17},{2,18},{3,19},{4,20},{5,21},{6,22},{7,23},{8,24},{9,... | collective-permute-start | bytes 1572872 | tf_op jit(solution)/shard_map/ppermute | solution.py:20
  168.7 29.9 %collective-permute-start.11 = (bf16[1024,256]{0,1:T(8,128)(2,1)S(1)}, bf16[1024,256]{0,1:T(8,128)(2,1)S(1)}, u32[]{:S(2)}, u32[]{:S(2)}) collective-permute-start(bf16[1024,256]{0,1:T(8,128)(2,1)S(1)} %broadcast_select_fusion.7), channel_id=1, source_target_pairs={{0,4},{1,5},{2,6},{3,7},{4,0},{5,1},{6,2},{7,3},{8,12},{9,13},{10,... | collective-permute-start | bytes 1572872 | tf_op jit(solution)/shard_map/ppermute | solution.py:14
  198.6 12.0 %collective-permute-start.12 = (bf16[1024,256]{0,1:T(8,128)(2,1)S(1)}, bf16[1024,256]{0,1:T(8,128)(2,1)S(1)}, u32[]{:S(2)}, u32[]{:S(2)}) collective-permute-start(bf16[1024,256]{0,1:T(8,128)(2,1)S(1)} %collective-permute-done.11), channel_id=1, source_target_pairs={{0,32},{1,33},{2,34},{3,35},{4,36},{5,37},{6,38},{7,39},{8,40},{9,... | collective-permute-start | bytes 1572872 | tf_op jit(solution)/shard_map/ppermute | solution.py:14
  210.7 27.5 %collective-permute-start.13 = (bf16[1024,256]{0,1:T(8,128)(2,1)S(1)}, bf16[1024,256]{0,1:T(8,128)(2,1)S(1)}, u32[]{:S(2)}, u32[]{:S(2)}) collective-permute-start(bf16[1024,256]{0,1:T(8,128)(2,1)S(1)} %broadcast_select_fusion), channel_id=1, source_target_pairs={{0,8},{1,9},{2,10},{3,11},{4,12},{5,13},{6,14},{7,15},{8,0},{9,1},... | collective-permute-start | bytes 1572872 | tf_op jit(solution)/shard_map/ppermute | solution.py:14
  238.2 12.3 %collective-permute-start.14 = (bf16[1024,256]{0,1:T(8,128)(2,1)S(1)}, bf16[1024,256]{0,1:T(8,128)(2,1)S(1)}, u32[]{:S(2)}, u32[]{:S(2)}) collective-permute-start(bf16[1024,256]{0,1:T(8,128)(2,1)S(1)} %collective-permute-done.13), channel_id=1, source_target_pairs={{0,64},{1,65},{2,66},{3,67},{4,68},{5,69},{6,70},{7,71},{8,72},{9,... | collective-permute-start | bytes 1572872 | tf_op jit(solution)/shard_map/ppermute | solution.py:14
  250.5 28.9 %collective-permute-start.15 = (bf16[1024,256]{0,1:T(8,128)(2,1)S(1)}, bf16[1024,256]{0,1:T(8,128)(2,1)S(1)}, u32[]{:S(2)}, u32[]{:S(2)}) collective-permute-start(bf16[1024,256]{0,1:T(8,128)(2,1)S(1)} %broadcast_select_fusion.2), channel_id=1, source_target_pairs={{0,16},{1,17},{2,18},{3,19},{4,20},{5,21},{6,22},{7,23},{8,24},{9,... | collective-permute-start | bytes 1572872 | tf_op jit(solution)/shard_map/ppermute | solution.py:14
  279.4 14.3 %collective-permute-start.16 = (bf16[1024,256]{0,1:T(8,128)(2,1)S(1)}, bf16[1024,256]{0,1:T(8,128)(2,1)S(1)}, u32[]{:S(2)}, u32[]{:S(2)}) collective-permute-start(bf16[1024,256]{0,1:T(8,128)(2,1)S(1)} %collective-permute-done.15), channel_id=1, source_target_pairs={{0,128},{1,129},{2,130},{3,131},{4,132},{5,133},{6,134},{7,135},{8... | collective-permute-start | bytes 1572872 | tf_op jit(solution)/shard_map/ppermute | solution.py:14
  279.5 15.0 %collective-permute-start.17 = (bf16[1024,256]{0,1:T(8,128)(2,1)S(1)}, bf16[1024,256]{0,1:T(8,128)(2,1)S(1)}, u32[]{:S(2)}, u32[]{:S(2)}) collective-permute-start(bf16[1024,256]{0,1:T(8,128)(2,1)S(1)} %broadcast_select_fusion.7), channel_id=1, source_target_pairs={{0,28},{1,29},{2,30},{3,31},{4,0},{5,1},{6,2},{7,3},{8,4},{9,5},{1... | collective-permute-start | bytes 1572872 | tf_op jit(solution)/shard_map/ppermute | solution.py:20
  293.8 12.9 %collective-permute-start.18 = (bf16[256,1024]{1,0:T(8,128)(2,1)S(1)}, bf16[256,1024]{1,0:T(8,128)(2,1)S(1)}, u32[]{:S(2)}, u32[]{:S(2)}) collective-permute-start(bf16[256,1024]{1,0:T(8,128)(2,1)S(1)} %fusion.2), channel_id=1, source_target_pairs={{0,224},{32,0},{64,32},{96,64},{128,96},{160,128},{192,160},{224,1... | collective-permute-start | bytes 1572872 | tf_op jit(solution)/shard_map/ppermute | solution.py:20
where the time goes:
time: 313 us; the launch traced here: 310 us
  waiting for transfers between devices  247 us (79%)
  starting transfers between devices  54.6 us (17%)
  matrix products  3.53 us (1%)
    ppermute x14, waiting for transfers between devices, swapped(): return lax.ppermute(value, axis, pairs)  198 us
    ppermute x5, waiting for transfers between devices, from_behind(): return lax.ppermute(value, axis, pairs)  49.4 us
    ppermute x14, starting transfers between devices, swapped(): return lax.ppermute(value, axis, pairs)  36 us
    ppermute x5, starting transfers between devices, from_behind(): return lax.ppermute(value, axis, pairs)  18.6 us
  transfers between devices with their start and end apart: 19, of which 18 were waited for; matrix products, arithmetic and copies ran while one was open for 0% of the time, Pallas kernels for 0%

commit v1 on v0

v1 whole, which is shorter than its diff:
```python
import jax
import jax.numpy as jnp
from jax import lax
from jax.experimental import pallas as pl
from jax.experimental.pallas import tpu as pltpu
from jax.sharding import PartitionSpec as P

TILE = 64
GROUPS = 4
ROWS = 8
STEPS = 2
MESH = pl.DeviceIdType.MESH


def wrap(index):
    return lax.rem(index + 2 * ROWS, ROWS)


def remote(source, target, send_sem, recv_sem, row, block, group):
    return pltpu.make_async_remote_copy(
        src_ref=source,
        dst_ref=target,
        send_sem=send_sem,
        recv_sem=recv_sem,
        device_id={"row": row, "col": block * GROUPS + group},
        device_id_type=MESH,
    )


def spread_kernel(
    upper_ref,
    left_ref,
    right_ref,
    piece,
    mirror,
    mirror_send,
    mirror_recv,
    left_send,
    left_recv,
    right_send,
    right_recv,
    local_sem,
):
    row = lax.axis_index("row")
    col = lax.axis_index("col")
    block = lax.div(col, GROUPS)
    group = lax.rem(col, GROUPS)
    width = upper_ref.shape[1]
    is_upper = row < block
    is_lower = row > block
    is_diag = row == block

    def quarter(ref, g):
        return ref.at[pl.ds(g * width, width), :]

    def greet(r, b, g):
        pl.semaphore_signal(
            barrier,
            inc=1,
            device_id={"row": r, "col": b * GROUPS + g},
            device_id_type=MESH,
        )

    barrier = pltpu.get_barrier_semaphore()
    for g in range(GROUPS):

        @pl.when(is_lower | (is_diag & (group != g)))
        def _(g=g):
            greet(block, row, g)

        for s in range(STEPS):

            @pl.when((wrap(block + s) != 0) | (group != g))
            def _(g=g, s=s):
                greet(wrap(row + block + s), block, g)

    for s in range(STEPS):

        @pl.when(wrap(row + s) != 0)
        def _(s=s):
            greet(row, wrap(row + block + s), group)

    count = jnp.int32(0)
    count += jnp.where(is_upper, GROUPS, jnp.where(is_diag, GROUPS - 1, 0))
    for s in range(STEPS):
        count += jnp.where(wrap(row + s) != 0, 1, 0)
        count += jnp.where(wrap(block + s) != 0, GROUPS, GROUPS - 1)
    pl.semaphore_wait(barrier, count)

    def mirror_copy(g):
        return remote(
            quarter(upper_ref, g),
            mirror.at[group],
            mirror_send.at[g],
            mirror_recv.at[group],
            block,
            row,
            g,
        )

    def mirror_arrival(g):
        return remote(
            quarter(upper_ref, g),
            mirror.at[g],
            mirror_send.at[g],
            mirror_recv.at[g],
            block,
            row,
            g,
        )

    for g in range(GROUPS):

        @pl.when(is_upper | (is_diag & (group != g)))
        def _(g=g):
            mirror_copy(g).start()

    def left_copy(source, s):
        return remote(
            source,
            left_ref.at[s],
            left_send.at[s],
            left_recv.at[s],
            row,
            wrap(block - row - s),
            group,
        )

    def right_copy(source, s, g):
        return remote(
            quarter(source, g),
            right_ref.at[s, group],
            right_send.at[s, g],
            right_recv.at[s, group],
            wrap(row - block - s),
            block,
            g,
        )

    def right_arrival(s, g):
        return remote(
            quarter(piece, g),
            right_ref.at[s, g],
            right_send.at[s, g],
            right_recv.at[s, g],
            wrap(row - block - s),
            block,
            g,
        )

    def local_left(source, s):
        return pltpu.make_async_copy(source, left_ref.at[s], local_sem.at[0, s])

    def local_right(source, s):
        return pltpu.make_async_copy(
            quarter(source, group), right_ref.at[s, group], local_sem.at[1, s]
        )

    def send_all(source):
        for s in range(STEPS):
            stays = wrap(row + s) == 0

            @pl.when(stays)
            def _(s=s):
                local_left(source, s).start()

            @pl.when(jnp.logical_not(stays))
            def _(s=s):
                left_copy(source, s).start()

            for g in range(GROUPS):
                home = (wrap(block + s) == 0) & (group == g)

                @pl.when(home)
                def _(s=s):
                    local_right(source, s).start()

                @pl.when(jnp.logical_not(home))
                def _(s=s, g=g):
                    right_copy(source, s, g).start()

    @pl.when(is_upper)
    def _():
        send_all(upper_ref)

    for g in range(GROUPS):

        @pl.when(is_lower | (is_diag & (group != g)))
        def _(g=g):
            mirror_arrival(g).wait_recv()

        @pl.when(is_lower)
        def _(g=g):
            piece[pl.ds(g * width, width), :] = mirror[g].T

        @pl.when(is_diag & (group != g))
        def _(g=g):
            here = upper_ref[pl.ds(g * width, width), :].astype(jnp.float32)
            there = mirror[g].T.astype(jnp.float32)
            piece[pl.ds(g * width, width), :] = (here + there).astype(jnp.bfloat16)

        @pl.when(is_diag & (group == g))
        def _(g=g):
            here = upper_ref[pl.ds(g * width, width), :]
            there = here.T.astype(jnp.float32)
            piece[pl.ds(g * width, width), :] = (
                here.astype(jnp.float32) + there
            ).astype(jnp.bfloat16)

    @pl.when(jnp.logical_not(is_upper))
    def _():
        send_all(piece)

    for g in range(GROUPS):

        @pl.when(is_upper | (is_diag & (group != g)))
        def _(g=g):
            mirror_copy(g).wait_send()

    for s in range(STEPS):
        stays = wrap(row + s) == 0

        @pl.when(stays)
        def _(s=s):
            local_left(piece, s).wait()

        @pl.when(jnp.logical_not(stays))
        def _(s=s):
            left_copy(piece, s).wait()

        for g in range(GROUPS):
            home = (wrap(block + s) == 0) & (group == g)

            @pl.when(home)
            def _(s=s):
                local_right(piece, s).wait()

            @pl.when(jnp.logical_not(home))
            def _(s=s, g=g):
                right_copy(piece, s, g).wait_send()
                right_arrival(s, g).wait_recv()


def product_kernel(left_ref, right_ref, out_ref):
    out_ref[...] = jnp.dot(
        left_ref[0], right_ref[0, 0], preferred_element_type=jnp.float32
    ) + jnp.dot(left_ref[1], right_ref[1, 0], preferred_element_type=jnp.float32)


def shards(tile_values, upper_mask):
    row = lax.axis_index("row")
    col = lax.axis_index("col")
    height, width = tile_values.shape
    tiles_high = height // TILE
    tiles_wide = width // TILE
    tile_rows = row * tiles_high + jnp.arange(tiles_high, dtype=jnp.int32)
    tile_cols = col * tiles_wide + jnp.arange(tiles_wide, dtype=jnp.int32)
    keep = (upper_mask != 0) & (tile_rows[:, None] <= tile_cols[None, :])
    keep_cells = jnp.repeat(jnp.repeat(keep, TILE, axis=0), TILE, axis=1)
    upper = jnp.where(keep_cells, tile_values, jnp.zeros_like(tile_values))
    vmem = pl.BlockSpec(memory_space=pltpu.VMEM)
    dma = pltpu.SemaphoreType.DMA
    left, right = pl.pallas_call(
        spread_kernel,
        out_shape=(
            jax.ShapeDtypeStruct((STEPS, height, width), jnp.bfloat16),
            jax.ShapeDtypeStruct((STEPS, GROUPS, width, width), jnp.bfloat16),
        ),
        in_specs=[vmem],
        out_specs=(vmem, vmem),
        scratch_shapes=[
            pltpu.VMEM((height, width), jnp.bfloat16),
            pltpu.VMEM((GROUPS, width, width), jnp.bfloat16),
            dma((GROUPS,)),
            dma((GROUPS,)),
            dma((STEPS,)),
            dma((STEPS,)),
            dma((STEPS, GROUPS)),
            dma((STEPS, GROUPS)),
            dma((2, STEPS)),
        ],
        compiler_params=pltpu.CompilerParams(collective_id=0, has_side_effects=True),
    )(upper)
    return pl.pallas_call(
        product_kernel,
        grid=(GROUPS,),
        out_shape=jax.ShapeDtypeStruct((height, height), jnp.float32),
        in_specs=[
            pl.BlockSpec((STEPS, height, width), lambda g: (0, 0, 0)),
            pl.BlockSpec((STEPS, 1, width, width), lambda g: (0, g, 0, 0)),
        ],
        out_specs=pl.BlockSpec((height, width), lambda g: (0, g)),
    )(left, right)


def solution(mesh):
    in_specs = (P("row", "col"), P("row", "col"))
    out_specs = P("row", "col")
    return jax.shard_map(
        shards, mesh=mesh, in_specs=in_specs, out_specs=out_specs, check_vma=False
    )
```

time: 313 us -> 123 us (0.39)
  the two profiles are of different devices: /device:TPU:23 before, /device:TPU:43 now
where the time goes in v1:
time: 123 us
  Pallas kernels  120 us (98%)
  other arithmetic  2.65 us (2%)
    pallas_call x1, Pallas kernels, shards(): pl.pallas_call(spread_kernel, out_shape=(jax.ShapeDtypeStruct((STEPS, hei...  115 us
    pallas_call x1, Pallas kernels, shards(): pl.pallas_call(product_kernel, grid=(GROUPS,), out_shape=jax.ShapeDtypeSt...  5.11 us

profile of v1, /device:TPU:43, one launch (start us, length us, event | category | flops | bytes accessed | tf_op | source)
XLA Modules:
  0.0 123.0 jit_solution(14130674857844570426)
XLA Ops:
  0.0 0.8 compare_and_fusion
  0.8 0.1 broadcast_in_dim.11
  0.8 0.1 reshape.14
  0.9 0.1 broadcast_in_dim.12
  1.0 0.4 copy.4
  1.5 1.9 %broadcast_select_fusion.upper_ref = bf16[1024,256]{1,0:T(8,128)(2,1)} fusion(pred[1024,256]{1,0:T(8,128)(4,1)S(1)} %copy.4, bf16[1024,256]{1,0:T(8,128)(2,1)} %param.2), kind=kLoop, calls=%fused_computation | loop fusion | flops 262144 | bytes 1310720 | tf_op jit(solution)/shard_map/jit(_where)/select_n | solution.py:260
  3.4 114.6 %shard_map.28 = (bf16[2,1024,256]{2,1,0:T(8,128)(2,1)}, bf16[2,4,256,256]{3,2,1,0:T(8,128)(2,1)}) custom-call(bf16[1024,256]{1,0:T(8,128)(2,1)} %broadcast_select_fusion.upper_ref), custom_call_target="tpu_custom_call" | custom-call | tf_op jit(solution)/shard_map/pallas_call | solution.py:263
  117.9 5.1 %shard_map.29 = f32[1024,1024]{1,0:T(8,128)} custom-call(bf16[2,1024,256]{2,1,0:T(8,128)(2,1)} %get-tuple-element.7.left_ref, bf16[2,4,256,256]{3,2,1,0:T(8,128)(2,1)} %get-tuple-element.8.right_ref), custom_call_target="tpu_custom_call" | custom-call | tf_op jit(solution)/shard_map/pallas_call | solution.py:284
  (2 shorter events, 0.0 us)

commit v2 on v1

v2 whole, which is shorter than its diff:
```python
import jax
import jax.numpy as jnp
from jax import lax
from jax.experimental import pallas as pl
from jax.experimental.pallas import tpu as pltpu
from jax.sharding import PartitionSpec as P

TILE = 64
GROUPS = 4
ROWS = 8
STEPS = 2
MESH = pl.DeviceIdType.MESH

RELAY = (
    (
        (0, 0, 7, 5, 0, 1, 0, 2),
        (0, 0, 3, 1, 0, 0, 7, 1),
        (0, 0, 0, 4, 2, 2, 7, 4),
        (0, 0, 0, 0, 4, 4, 7, 5),
        (0, 0, 0, 0, 0, 5, 6, 3),
        (0, 0, 0, 0, 0, 0, 7, 7),
        (0, 0, 0, 0, 0, 0, 0, 7),
        (0, 0, 0, 0, 0, 0, 0, 0),
    ),
    (
        (0, 6, 5, 7, 1, 0, 2, 3),
        (0, 0, 0, 2, 7, 0, 1, 4),
        (0, 0, 0, 3, 5, 7, 0, 7),
        (0, 0, 0, 0, 3, 5, 7, 6),
        (0, 0, 0, 0, 0, 5, 7, 6),
        (0, 0, 0, 0, 0, 0, 3, 6),
        (0, 0, 0, 0, 0, 0, 0, 7),
        (0, 0, 0, 0, 0, 0, 0, 0),
    ),
)
FROM_MIRROR = (
    (0, 0, 1, 0, 0, 0, 0, 0),
    (0, 0, 0, 0, 0, 0, 0, 0),
    (1, 0, 0, 0, 1, 1, 0, 0),
    (0, 1, 1, 0, 1, 0, 0, 1),
    (0, 0, 0, 1, 0, 1, 1, 0),
    (0, 0, 0, 1, 0, 0, 1, 0),
    (0, 0, 0, 0, 0, 0, 0, 0),
    (0, 0, 0, 0, 0, 0, 0, 0),
)
FIRST = (
    (0, 0, 1, 0, 0, 0, 0, 0),
    (0, 0, 0, 0, 0, 0, 0, 0),
    (1, 0, 0, 0, 1, 1, 0, 0),
    (1, 0, 1, 0, 0, 0, 1, 0),
    (1, 0, 1, 1, 1, 0, 1, 0),
    (1, 1, 1, 0, 1, 1, 0, 1),
    (1, 1, 1, 1, 1, 1, 1, 1),
    (1, 1, 1, 1, 1, 1, 1, 1),
)


def wrap(index):
    return lax.rem(index + 2 * ROWS, ROWS)


def word_of(entries):
    return sum(entry * 8**place for place, entry in enumerate(entries))


def look(table, i, j):
    if isinstance(i, int):
        word = jnp.int32(word_of(table[i]))
    else:
        word = jnp.int32(word_of(table[0]))
        for k in range(1, ROWS):
            word = jnp.where(i == k, jnp.int32(word_of(table[k])), word)
    return lax.rem(lax.shift_right_logical(word, 3 * j), 8)


def spread_kernel(
    values_ref,
    mask_ref,
    left_ref,
    right_ref,
    piece,
    mirror,
    passing,
    held,
    relay_send,
    relay_recv,
    pass_send,
    mirror_send,
    mirror_recv,
    direct_send,
    turned_send,
    forward_send,
    left_recv,
    right_send,
    right_recv,
):
    row = lax.axis_index("row")
    col = lax.axis_index("col")
    block = lax.div(col, GROUPS)
    group = lax.rem(col, GROUPS)
    width = values_ref.shape[1]
    is_upper = row < block
    is_lower = row > block
    is_diag = row == block

    relay = [look(RELAY[p], row, block) for p in range(2)]
    back_relay = [look(RELAY[p], block, row) for p in range(2)]
    back_row = jnp.where(lax.rem(group, 2) == 0, back_relay[0], back_relay[1])
    back_row = jnp.where(is_diag, row, back_row)
    passes = {
        (a, p): (look(RELAY[p], a, block) == row) & (a < block) & (row != a)
        for a in range(ROWS)
        for p in range(2)
    }
    own_mirror = look(FROM_MIRROR, row, block) == 1
    own_first = look(FIRST, row, block)
    own_target = wrap(block - row - own_first)
    back_mirror = look(FROM_MIRROR, block, row) == 1
    back_first = look(FIRST, block, row)
    back_target = wrap(row - block - back_first)
    inner = [wrap(row + block + s) for s in range(STEPS)]
    first_here = [look(FIRST, row, inner[s]) == s for s in range(STEPS)]
    turned = [look(FROM_MIRROR, row, inner[s]) == 1 for s in range(STEPS)]

    def quarter(ref, g):
        return ref.at[pl.ds(g * width, width), :]

    def remote(source, target, send_sem, recv_sem, r, b, g):
        return pltpu.make_async_remote_copy(
            src_ref=source,
            dst_ref=target,
            send_sem=send_sem,
            recv_sem=recv_sem,
            device_id={"row": r, "col": b * GROUPS + g},
            device_id_type=MESH,
        )

    barrier = pltpu.get_barrier_semaphore()

    def greet(r, b, g):
        pl.semaphore_signal(
            barrier,
            inc=1,
            device_id={"row": r, "col": b * GROUPS + g},
            device_id_type=MESH,
        )

    count = jnp.int32(0)

    def expect(condition, amount):
        return count + jnp.where(condition, amount, 0)

    for a in range(ROWS):
        for p in range(2):

            @pl.when(passes[a, p])
            def _(a=a):
                greet(a, block, group)

            count = expect(passes[a, p], 2)
    for p in range(2):
        count = expect(is_upper & (relay[p] != row), 1)
        count = expect(is_upper & (relay[p] == row), 2)
    count = expect(is_diag, GROUPS - 1)
    for g in range(GROUPS):

        @pl.when(is_lower | (is_diag & (group != g)))
        def _(g=g):
            greet(back_row, row, g)

        for s in range(STEPS):
            home = (wrap(block + s) == 0) & (group == g)

            @pl.when(jnp.logical_not(home))
            def _(g=g, s=s):
                greet(inner[s], block, g)

            count = expect(jnp.logical_not(home), 1)
        count = expect(back_mirror, 1)
    count = expect(jnp.logical_not(own_mirror) & (own_target != block), 1)
    for s in range(STEPS):
        neighbour = wrap(block - 1 + 2 * s)
        straight = first_here[s] & jnp.logical_not(turned[s]) & (inner[s] != block)

        @pl.when(straight)
        def _(s=s):
            greet(row, inner[s], group)

        for g in range(GROUPS):

            @pl.when(first_here[s] & turned[s])
            def _(g=g, s=s):
                greet(inner[s], row, g)

        count = expect(first_here[s], 1)
        source = wrap(block + 1 - 2 * (1 - s))

        @pl.when(jnp.logical_not(first_here[s]))
        def _(source=source):
            greet(row, source, group)

    @pl.when(jnp.logical_not(is_lower))
    def _():
        lane_tile = lax.div(lax.broadcasted_iota(jnp.int32, (1, width), 1), TILE)
        tiles_wide = width // TILE
        tiles_high = values_ref.shape[0] // TILE
        for i in range(tiles_high):
            marks = jnp.zeros((1, width), jnp.int32)
            for j in range(tiles_wide):
                marks = jnp.where(lane_tile == j, mask_ref[i : i + 1, j : j + 1], marks)
            ahead = row * tiles_high + i <= col * tiles_wide + lane_tile
            keep = jnp.where((marks != 0) & ahead, 1.0, 0.0)
            keep = jnp.broadcast_to(keep, (TILE, width)) > 0.5
            rows = pl.ds(i * TILE, TILE)
            tile = values_ref[rows, :].astype(jnp.float32)
            piece[rows, :] = jnp.where(keep, tile, 0.0).astype(jnp.bfloat16)

    pl.semaphore_wait(barrier, count)

    def relay_copy(a, g):
        return remote(
            quarter(piece, g),
            passing.at[a, g],
            relay_send.at[g],
            relay_recv.at[a, g],
            relay[g % 2],
            block,
            group,
        )

    def mirror_copy(g):
        return remote(
            quarter(piece, g),
            mirror.at[group],
            mirror_send.at[g],
            mirror_recv.at[group],
            block,
            row,
            g,
        )

    def pass_copy(a, g):
        return remote(
            passing.at[a, g],
            mirror.at[group],
            pass_send.at[a, g],
            mirror_recv.at[group],
            block,
            a,
            g,
        )

    def mirror_arrival(g):
        return remote(
            quarter(piece, g),
            mirror.at[g],
            mirror_send.at[g],
            mirror_recv.at[g],
            block,
            row,
            g,
        )

    by_relay = [is_upper & (relay[p] != row) for p in range(2)]
    by_self = [is_upper & (relay[p] == row) for p in range(2)]

    for g in range(GROUPS):

        @pl.when(by_relay[g % 2])
        def _(g=g):
            relay_copy(row, g).start()

        @pl.when(by_self[g % 2] | (is_diag & (group != g)))
        def _(g=g):
            mirror_copy(g).start()

    def direct_copy(q):
        return remote(
            quarter(piece, q),
            held.at[own_first, q],
            direct_send.at[q],
            left_recv.at[own_first, q],
            row,
            own_target,
            group,
        )

    def direct_local(q):
        return pltpu.make_async_copy(
            quarter(piece, q), held.at[own_first, q], left_recv.at[own_first, q]
        )

    def turned_copy(q):
        return remote(
            quarter(piece, q),
            held.at[back_first, group],
            turned_send.at[q],
            left_recv.at[back_first, group],
            block,
            back_target,
            q,
        )

    def right_copy(s, q):
        return remote(
            quarter(piece, q),
            right_ref.at[s, group],
            right_send.at[s, q],
            right_recv.at[s, group],
            wrap(row - block - s),
            block,
            q,
        )

    def right_local(s, q):
        return pltpu.make_async_copy(
            quarter(piece, q), right_ref.at[s, group], right_recv.at[s, group]
        )

    own_far = jnp.logical_not(own_mirror) & (own_target != block)
    own_home = jnp.logical_not(own_mirror) & (own_target == block)

    def send_quarter(q):
        @pl.when(own_far)
        def _():
            direct_copy(q).start()

        @pl.when(own_home)
        def _():
            direct_local(q).start()

        @pl.when(back_mirror)
        def _():
            turned_copy(q).start()

        for s in range(STEPS):
            home = (wrap(block + s) == 0) & (group == q)

            @pl.when(home)
            def _(s=s):
                right_local(s, q).start()

            @pl.when(jnp.logical_not(home))
            def _(s=s):
                right_copy(s, q).start()

    @pl.when(is_upper)
    def _():
        for q in range(GROUPS):
            send_quarter(q)

    for a in range(ROWS):
        for g in range(GROUPS):

            @pl.when(passes[a, g % 2])
            def _(a=a, g=g):
                relay_copy(a, g).wait_recv()
                pass_copy(a, g).start()

    @pl.when(jnp.logical_not(is_upper))
    def _():
        for g in range(GROUPS):
            rows = pl.ds(g * width, width)

            @pl.when(is_lower)
            def _(g=g, rows=rows):
                mirror_arrival(g).wait_recv()
                piece[rows, :] = mirror[g].T

            @pl.when(is_diag & (group != g))
            def _(g=g, rows=rows):
                mirror_arrival(g).wait_recv()
                mirror_copy(g).wait_send()
                here = piece[rows, :].astype(jnp.float32)
                there = mirror[g].T.astype(jnp.float32)
                piece[rows, :] = (here + there).astype(jnp.bfloat16)

            @pl.when(is_diag & (group == g))
            def _(g=g, rows=rows):
                here = piece[rows, :]
                there = here.T.astype(jnp.float32)
                piece[rows, :] = (here.astype(jnp.float32) + there).astype(jnp.bfloat16)

            send_quarter(g)

    def forward_copy(s, q):
        return remote(
            held.at[s, q],
            held.at[1 - s, q],
            forward_send.at[s, q],
            left_recv.at[1 - s, q],
            row,
            wrap(block - 1 + 2 * s),
            group,
        )

    def left_arrival(s, q):
        return remote(
            quarter(piece, q),
            held.at[s, q],
            direct_send.at[q],
            left_recv.at[s, q],
            row,
            own_target,
            group,
        )

    def settle(s, q):
        rows = pl.ds(q * width, width)

        @pl.when(turned[s])
        def _():
            left_ref[s, rows, :] = held[s, q].T

        @pl.when(jnp.logical_not(turned[s]))
        def _():
            left_ref[s, rows, :] = held[s, q]

    for q in range(GROUPS):
        for s in range(STEPS):

            @pl.when(first_here[s])
            def _(s=s, q=q):
                left_arrival(s, q).wait_recv()
                forward_copy(s, q).start()

    for q in range(GROUPS):
        for s in range(STEPS):

            @pl.when(jnp.logical_not(first_here[s]))
            def _(s=s, q=q):
                left_arrival(s, q).wait_recv()

            settle(s, q)

    for g in range(GROUPS):
        for s in range(STEPS):
            remote(
                quarter(piece, g),
                right_ref.at[s, g],
                right_send.at[s, g],
                right_recv.at[s, g],
                row,
                block,
                g,
            ).wait_recv()
            home = (wrap(block + s) == 0) & (group == g)

            @pl.when(jnp.logical_not(home))
            def _(s=s, g=g):
                right_copy(s, g).wait_send()

            @pl.when(first_here[s])
            def _(s=s, g=g):
                forward_copy(s, g).wait_send()

        @pl.when(own_far)
        def _(g=g):
            direct_copy(g).wait_send()

        @pl.when(back_mirror)
        def _(g=g):
            turned_copy(g).wait_send()

        @pl.when(by_relay[g % 2])
        def _(g=g):
            relay_copy(row, g).wait_send()

        @pl.when(by_self[g % 2])
        def _(g=g):
            mirror_copy(g).wait_send()

        for a in range(ROWS):

            @pl.when(passes[a, g % 2])
            def _(a=a, g=g):
                pass_copy(a, g).wait_send()


def product_kernel(left_ref, right_ref, out_ref):
    out_ref[...] = jnp.dot(
        left_ref[0], right_ref[0, 0], preferred_element_type=jnp.float32
    ) + jnp.dot(left_ref[1], right_ref[1, 0], preferred_element_type=jnp.float32)


def shards(tile_values, upper_mask):
    height, width = tile_values.shape
    vmem = pl.BlockSpec(memory_space=pltpu.VMEM)
    dma = pltpu.SemaphoreType.DMA
    square = (width, width)
    left, right = pl.pallas_call(
        spread_kernel,
        out_shape=(
            jax.ShapeDtypeStruct((STEPS, height, width), jnp.bfloat16),
            jax.ShapeDtypeStruct((STEPS, GROUPS) + square, jnp.bfloat16),
        ),
        in_specs=[vmem, vmem],
        out_specs=(vmem, vmem),
        scratch_shapes=[
            pltpu.VMEM((height, width), jnp.bfloat16),
            pltpu.VMEM((GROUPS,) + square, jnp.bfloat16),
            pltpu.VMEM((ROWS, GROUPS) + square, jnp.bfloat16),
            pltpu.VMEM((STEPS, GROUPS) + square, jnp.bfloat16),
            dma((GROUPS,)),
            dma((ROWS, GROUPS)),
            dma((ROWS, GROUPS)),
            dma((GROUPS,)),
            dma((GROUPS,)),
            dma((GROUPS,)),
            dma((GROUPS,)),
            dma((STEPS, GROUPS)),
            dma((STEPS, GROUPS)),
            dma((STEPS, GROUPS)),
            dma((STEPS, GROUPS)),
        ],
        compiler_params=pltpu.CompilerParams(collective_id=0, has_side_effects=True),
    )(tile_values, upper_mask)
    return pl.pallas_call(
        product_kernel,
        grid=(GROUPS,),
        out_shape=jax.ShapeDtypeStruct((height, height), jnp.float32),
        in_specs=[
            pl.BlockSpec((STEPS, height, width), lambda g: (0, 0, 0)),
            pl.BlockSpec((STEPS, 1, width, width), lambda g: (0, g, 0, 0)),
        ],
        out_specs=pl.BlockSpec((height, width), lambda g: (0, g)),
    )(left, right)


def solution(mesh):
    in_specs = (P("row", "col"), P("row", "col"))
    out_specs = P("row", "col")
    return jax.shard_map(
        shards, mesh=mesh, in_specs=in_specs, out_specs=out_specs, check_vma=False
    )
```

time: 123 us -> 87.9 us (0.71)
  the two profiles are of different devices: /device:TPU:43 before, /device:TPU:23 now
where the time goes in v2:
time: 87.9 us; the launch traced here: 87.7 us
  Pallas kernels  86.4 us (98%)
  local copies, waits for them, and re-layouts  1.35 us (2%)
    pallas_call x1, Pallas kernels, shards(): pl.pallas_call(spread_kernel, out_shape=(jax.ShapeDtypeStruct((STEPS, hei...  81.3 us
    pallas_call x1, Pallas kernels, shards(): pl.pallas_call(product_kernel, grid=(GROUPS,), out_shape=jax.ShapeDtypeSt...  5.12 us

profile of v2, /device:TPU:23, one launch (start us, length us, event | category | flops | bytes accessed | tf_op | source)
XLA Modules:
  0.0 87.7 jit_solution(10886510742287902335)
XLA Ops:
  0.0 1.4 %copy.3.mask_ref = s32[16,4]{1,0:T(8,128)} copy(s32[16,4]{0,1:T(4,128)} %param.3) | data formatting | bytes 512 | tf_op args[1]
  1.4 81.3 %shard_map.28 = (bf16[2,1024,256]{2,1,0:T(8,128)(2,1)}, bf16[2,4,256,256]{3,2,1,0:T(8,128)(2,1)}) custom-call(bf16[1024,256]{1,0:T(8,128)(2,1)} %values_ref.1, s32[16,4]{1,0:T(8,128)} %copy.3.mask_ref), custom_call_target="tpu_custom_call" | custom-call | tf_op jit(solution)/shard_map/pallas_call | solution.py:491
  82.6 5.1 %shard_map.29 = f32[1024,1024]{1,0:T(8,128)} custom-call(bf16[2,1024,256]{2,1,0:T(8,128)(2,1)} %get-tuple-element.7.left_ref, bf16[2,4,256,256]{3,2,1,0:T(8,128)(2,1)} %get-tuple-element.8.right_ref), custom_call_target="tpu_custom_call" | custom-call | tf_op jit(solution)/shard_map/pallas_call | solution.py:518

commit v3 on v2

--- a/solution.py
+++ b/solution.py
@@ -13,43 +13,63 @@
 
 RELAY = (
     (
-        (0, 0, 7, 5, 0, 1, 0, 2),
-        (0, 0, 3, 1, 0, 0, 7, 1),
-        (0, 0, 0, 4, 2, 2, 7, 4),
-        (0, 0, 0, 0, 4, 4, 7, 5),
-        (0, 0, 0, 0, 0, 5, 6, 3),
-        (0, 0, 0, 0, 0, 0, 7, 7),
+        (0, 6, 7, 4, 5, 2, 7, 1),
+        (0, 0, 7, 1, 3, 5, 7, 3),
+        (0, 0, 0, 0, 7, 4, 0, 4),
+        (0, 0, 0, 0, 5, 2, 5, 1),
+        (0, 0, 0, 0, 0, 2, 2, 0),
+        (0, 0, 0, 0, 0, 0, 3, 4),
+        (0, 0, 0, 0, 0, 0, 0, 4),
+        (0, 0, 0, 0, 0, 0, 0, 0),
+    ),
+    (
+        (0, 0, 1, 4, 2, 0, 2, 3),
+        (0, 0, 4, 7, 0, 2, 1, 7),
+        (0, 0, 0, 6, 2, 3, 5, 3),
+        (0, 0, 0, 0, 4, 4, 1, 6),
+        (0, 0, 0, 0, 0, 4, 7, 6),
+        (0, 0, 0, 0, 0, 0, 4, 7),
         (0, 0, 0, 0, 0, 0, 0, 7),
         (0, 0, 0, 0, 0, 0, 0, 0),
     ),
     (
-        (0, 6, 5, 7, 1, 0, 2, 3),
-        (0, 0, 0, 2, 7, 0, 1, 4),
-        (0, 0, 0, 3, 5, 7, 0, 7),
-        (0, 0, 0, 0, 3, 5, 7, 6),
-        (0, 0, 0, 0, 0, 5, 7, 6),
-        (0, 0, 0, 0, 0, 0, 3, 6),
-        (0, 0, 0, 0, 0, 0, 0, 7),
+        (0, 0, 2, 3, 3, 7, 5, 1),
+        (0, 0, 2, 2, 0, 6, 6, 0),
+        (0, 0, 0, 5, 7, 1, 0, 6),
+        (0, 0, 0, 0, 6, 3, 7, 5),
+        (0, 0, 0, 0, 0, 3, 3, 7),
+        (0, 0, 0, 0, 0, 0, 4, 2),
+        (0, 0, 0, 0, 0, 0, 0, 4),
+        (0, 0, 0, 0, 0, 0, 0, 0),
+    ),
+    (
+        (0, 2, 6, 1, 4, 2, 1, 6),
+        (0, 0, 3, 5, 6, 0, 6, 4),
+        (0, 0, 0, 3, 2, 4, 4, 5),
+        (0, 0, 0, 0, 3, 7, 0, 1),
+        (0, 0, 0, 0, 0, 5, 6, 0),
+        (0, 0, 0, 0, 0, 0, 3, 5),
+        (0, 0, 0, 0, 0, 0, 0, 6),
         (0, 0, 0, 0, 0, 0, 0, 0),
     ),
 )
 FROM_MIRROR = (
-    (0, 0, 1, 0, 0, 0, 0, 0),
     (0, 0, 0, 0, 0, 0, 0, 0),
-    (1, 0, 0, 0, 1, 1, 0, 0),
+    (0, 0, 0, 0, 0, 0, 0, 1),
+    (0, 1, 0, 0, 1, 1, 0, 1),
     (0, 1, 1, 0, 1, 0, 0, 1),
-    (0, 0, 0, 1, 0, 1, 1, 0),
-    (0, 0, 0, 1, 0, 0, 1, 0),
-    (0, 0, 0, 0, 0, 0, 0, 0),
+    (1, 0, 1, 1, 0, 1, 1, 0),
+    (0, 0, 0, 1, 1, 0, 0, 1),
+    (1, 0, 0, 0, 0, 0, 0, 0),
     (0, 0, 0, 0, 0, 0, 0, 0),
 )
 FIRST = (
-    (0, 0, 1, 0, 0, 0, 0, 0),
     (0, 0, 0, 0, 0, 0, 0, 0),
-    (1, 0, 0, 0, 1, 1, 0, 0),
-    (1, 0, 1, 0, 0, 0, 1, 0),
-    (1, 0, 1, 1, 1, 0, 1, 0),
-    (1, 1, 1, 0, 1, 1, 0, 1),
+    (0, 0, 0, 0, 0, 0, 0, 0),
+    (0, 1, 0, 0, 1, 1, 0, 0),
+    (0, 0, 1, 0, 1, 0, 1, 0),
+    (1, 1, 0, 0, 1, 0, 1, 0),
+    (1, 1, 1, 0, 0, 1, 1, 0),
     (1, 1, 1, 1, 1, 1, 1, 1),
     (1, 1, 1, 1, 1, 1, 1, 1),
 )
@@ -103,14 +123,16 @@
     is_lower = row > block
     is_diag = row == block
 
-    relay = [look(RELAY[p], row, block) for p in range(2)]
-    back_relay = [look(RELAY[p], block, row) for p in range(2)]
-    back_row = jnp.where(lax.rem(group, 2) == 0, back_relay[0], back_relay[1])
-    back_row = jnp.where(is_diag, row, back_row)
+    relay = [look(RELAY[g], row, block) for g in range(GROUPS)]
+    back_row = row
+    for g in range(GROUPS):
+        back_row = jnp.where(
+            is_lower & (group == g), look(RELAY[g], block, row), back_row
+        )
     passes = {
-        (a, p): (look(RELAY[p], a, block) == row) & (a < block) & (row != a)
+        (a, g): (look(RELAY[g], a, block) == row) & (a < block) & (row != a)
         for a in range(ROWS)
-        for p in range(2)
+        for g in range(GROUPS)
     }
     own_mirror = look(FROM_MIRROR, row, block) == 1
     own_first = look(FIRST, row, block)
@@ -125,6 +147,10 @@
     def quarter(ref, g):
         return ref.at[pl.ds(g * width, width), :]
 
+    def right_block(s, g):
+        place = g * width if isinstance(g, int) else pl.multiple_of(g * width, width)
+        return right_ref.at[pl.ds(s * width, width), pl.ds(place, width)]
+
     def remote(source, target, send_sem, recv_sem, r, b, g):
         return pltpu.make_async_remote_copy(
             src_ref=source,
@@ -151,16 +177,14 @@
         return count + jnp.where(condition, amount, 0)
 
     for a in range(ROWS):
-        for p in range(2):
-
-            @pl.when(passes[a, p])
+        for g in range(GROUPS):
+
+            @pl.when(passes[a, g])
             def _(a=a):
                 greet(a, block, group)
 
-            count = expect(passes[a, p], 2)
-    for p in range(2):
-        count = expect(is_upper & (relay[p] != row), 1)
-        count = expect(is_upper & (relay[p] == row), 2)
+            count = expect(passes[a, g], 1)
+    count = expect(is_upper, GROUPS)
     count = expect(is_diag, GROUPS - 1)
     for g in range(GROUPS):
 
@@ -207,7 +231,7 @@
         for i in range(tiles_high):
             marks = jnp.zeros((1, width), jnp.int32)
             for j in range(tiles_wide):
-                marks = jnp.where(lane_tile == j, mask_ref[i : i + 1, j : j + 1], marks)
+                marks = jnp.where(lane_tile == j, mask_ref[j : j + 1, i : i + 1], marks)
             ahead = row * tiles_high + i <= col * tiles_wide + lane_tile
             keep = jnp.where((marks != 0) & ahead, 1.0, 0.0)
             keep = jnp.broadcast_to(keep, (TILE, width)) > 0.5
@@ -223,7 +247,7 @@
             passing.at[a, g],
             relay_send.at[g],
             relay_recv.at[a, g],
-            relay[g % 2],
+            relay[g],
             block,
             group,
         )
@@ -261,16 +285,16 @@
             g,
         )
 
-    by_relay = [is_upper & (relay[p] != row) for p in range(2)]
-    by_self = [is_upper & (relay[p] == row) for p in range(2)]
+    by_relay = [is_upper & (relay[g] != row) for g in range(GROUPS)]
+    by_self = [is_upper & (relay[g] == row) for g in range(GROUPS)]
 
     for g in range(GROUPS):
 
-        @pl.when(by_relay[g % 2])
+        @pl.when(by_relay[g])
         def _(g=g):
             relay_copy(row, g).start()
 
-        @pl.when(by_self[g % 2] | (is_diag & (group != g)))
+        @pl.when(by_self[g] | (is_diag & (group != g)))
         def _(g=g):
             mirror_copy(g).start()
 
@@ -304,7 +328,7 @@
     def right_copy(s, q):
         return remote(
             quarter(piece, q),
-            right_ref.at[s, group],
+            right_block(s, group),
             right_send.at[s, q],
             right_recv.at[s, group],
             wrap(row - block - s),
@@ -314,13 +338,13 @@
 
     def right_local(s, q):
         return pltpu.make_async_copy(
-            quarter(piece, q), right_ref.at[s, group], right_recv.at[s, group]
+            quarter(piece, q), right_block(s, group), right_recv.at[s, group]
         )
 
     own_far = jnp.logical_not(own_mirror) & (own_target != block)
     own_home = jnp.logical_not(own_mirror) & (own_target == block)
 
-    def send_quarter(q):
+    def send_left(q):
         @pl.when(own_far)
         def _():
             direct_copy(q).start()
@@ -333,6 +357,7 @@
         def _():
             turned_copy(q).start()
 
+    def send_right(q):
         for s in range(STEPS):
             home = (wrap(block + s) == 0) & (group == q)
 
@@ -344,18 +369,20 @@
             def _(s=s):
                 right_copy(s, q).start()
 
+    for a in range(ROWS):
+        for g in range(GROUPS):
+
+            @pl.when(passes[a, g])
+            def _(a=a, g=g):
+                relay_copy(a, g).wait_recv()
+                pass_copy(a, g).start()
+
     @pl.when(is_upper)
     def _():
         for q in range(GROUPS):
-            send_quarter(q)
-
-    for a in range(ROWS):
-        for g in range(GROUPS):
-
-            @pl.when(passes[a, g % 2])
-            def _(a=a, g=g):
-                relay_copy(a, g).wait_recv()
-                pass_copy(a, g).start()
+            send_left(q)
+        for q in range(GROUPS):
+            send_right(q)
 
     @pl.when(jnp.logical_not(is_upper))
     def _():
@@ -381,7 +408,9 @@
                 there = here.T.astype(jnp.float32)
                 piece[rows, :] = (here.astype(jnp.float32) + there).astype(jnp.bfloat16)
 
-            send_quarter(g)
+            send_left(g)
+        for g in range(GROUPS):
+            send_right(g)
 
     def forward_copy(s, q):
         return remote(
@@ -410,11 +439,11 @@
 
         @pl.when(turned[s])
         def _():
-            left_ref[s, rows, :] = held[s, q].T
+            left_ref[rows, s * width : (s + 1) * width] = held[s, q].T
 
         @pl.when(jnp.logical_not(turned[s]))
         def _():
-            left_ref[s, rows, :] = held[s, q]
+            left_ref[rows, s * width : (s + 1) * width] = held[s, q]
 
     for q in range(GROUPS):
         for s in range(STEPS):
@@ -437,7 +466,7 @@
         for s in range(STEPS):
             remote(
                 quarter(piece, g),
-                right_ref.at[s, g],
+                right_block(s, g),
                 right_send.at[s, g],
                 right_recv.at[s, g],
                 row,
@@ -462,25 +491,21 @@
         def _(g=g):
             turned_copy(g).wait_send()
 
-        @pl.when(by_relay[g % 2])
-        def _(g=g):
-            relay_copy(row, g).wait_send()
-
-        @pl.when(by_self[g % 2])
-        def _(g=g):
-            mirror_copy(g).wait_send()
-
         for a in range(ROWS):
 
-            @pl.when(passes[a, g % 2])
+            @pl.when(passes[a, g])
             def _(a=a, g=g):
                 pass_copy(a, g).wait_send()
 
-
-def product_kernel(left_ref, right_ref, out_ref):
-    out_ref[...] = jnp.dot(
-        left_ref[0], right_ref[0, 0], preferred_element_type=jnp.float32
-    ) + jnp.dot(left_ref[1], right_ref[1, 0], preferred_element_type=jnp.float32)
+    for g in range(GROUPS):
+
+        @pl.when(by_relay[g])
+        def _(g=g):
+            relay_copy(row, g).wait_send()
+
+        @pl.when(by_self[g])
+        def _(g=g):
+            mirror_copy(g).wait_send()
 
 
 def shards(tile_values, upper_mask):
@@ -491,8 +516,8 @@
     left, right = pl.pallas_call(
         spread_kernel,
         out_shape=(
-            jax.ShapeDtypeStruct((STEPS, height, width), jnp.bfloat16),
-            jax.ShapeDtypeStruct((STEPS, GROUPS) + square, jnp.bfloat16),
+            jax.ShapeDtypeStruct((height, STEPS * width), jnp.bfloat16),
+            jax.ShapeDtypeStruct((STEPS * width, height), jnp.bfloat16),
         ),
         in_specs=[vmem, vmem],
         out_specs=(vmem, vmem),
@@ -514,17 +539,8 @@
             dma((STEPS, GROUPS)),
         ],
         compiler_params=pltpu.CompilerParams(collective_id=0, has_side_effects=True),
-    )(tile_values, upper_mask)
-    return pl.pallas_call(
-        product_kernel,
-        grid=(GROUPS,),
-        out_shape=jax.ShapeDtypeStruct((height, height), jnp.float32),
-        in_specs=[
-            pl.BlockSpec((STEPS, height, width), lambda g: (0, 0, 0)),
-            pl.BlockSpec((STEPS, 1, width, width), lambda g: (0, g, 0, 0)),
-        ],
-        out_specs=pl.BlockSpec((height, width), lambda g: (0, g)),
-    )(left, right)
+    )(tile_values, upper_mask.T)
+    return jnp.dot(left, right, preferred_element_type=jnp.float32)
 
 
 def solution(mesh):

time: 87.9 us -> 77.2 us (0.88)
  Pallas kernels: 86.4 us -> 72.3 us
  matrix products: 0 us -> 4.81 us
  local copies, waits for them, and re-layouts: 1.35 us -> 0 us
    pallas_call x2 -> x1, Pallas kernels: 86.4 us -> 72.3 us  [shards(): pl.pallas_call(spread_kernel, out_shape=(jax.ShapeDtypeStruct((height, ST...]
    dot_general x0 -> x1, matrix products: none -> 4.81 us  [shards(): return jnp.dot(left, right, preferred_element_type=jnp.float32)]
    unnamed x1 -> x0, local copies, waits for them, and re-layouts: 1.35 us -> none
where the time goes in v3:
time: 77.2 us; the launch traced here: 77.1 us
  Pallas kernels  72.3 us (94%)
  matrix products  4.81 us (6%)
    pallas_call x1, Pallas kernels, shards(): pl.pallas_call(spread_kernel, out_shape=(jax.ShapeDtypeStruct((height, ST...  72.3 us
    dot_general x1, matrix products, shards(): return jnp.dot(left, right, preferred_element_type=jnp.float32)  4.81 us

profile of v3, /device:TPU:23, one launch (start us, length us, event | category | flops | bytes accessed | tf_op | source)
XLA Modules:
  0.0 77.1 jit_solution(517868556406143410)
XLA Ops:
  0.0 72.3 %shard_map.28 = (bf16[1024,512]{1,0:T(8,128)(2,1)}, bf16[512,1024]{1,0:T(8,128)(2,1)}) custom-call(bf16[1024,256]{1,0:T(8,128)(2,1)} %values_ref.1, s32[4,16]{1,0:T(4,128)} %bitcast.3), custom_call_target="tpu_custom_call" | custom-call | tf_op jit(solution)/shard_map/pallas_call | solution.py:516
  72.3 4.8 %fusion = f32[1024,1024]{1,0:T(8,128)} fusion(bf16[1024,512]{1,0:T(8,128)(2,1)} %get-tuple-element.7, bf16[512,1024]{1,0:T(8,128)(2,1)} %get-tuple-element.8), kind=kOutput, calls=%fused_computation | convolution fusion | flops 1073741824 | bytes 6291456 | tf_op jit(solution)/shard_map/dot_general | solution.py:543

commit v4 on v3

--- a/solution.py
+++ b/solution.py
@@ -369,8 +369,8 @@
             def _(s=s):
                 right_copy(s, q).start()
 
-    for a in range(ROWS):
-        for g in range(GROUPS):
+    for g in range(GROUPS):
+        for a in range(ROWS):
 
             @pl.when(passes[a, g])
             def _(a=a, g=g):

time: 77.2 us -> 72.7 us (0.942)
  the two profiles are of different devices: /device:TPU:23 before, /device:TPU:119 now
where the time goes in v4:
time: 72.7 us; the launch traced here: 72.5 us
  Pallas kernels  67.7 us (93%)
  matrix products  4.81 us (7%)
    pallas_call x1, Pallas kernels, shards(): pl.pallas_call(spread_kernel, out_shape=(jax.ShapeDtypeStruct((height, ST...  67.7 us
    dot_general x1, matrix products, shards(): return jnp.dot(left, right, preferred_element_type=jnp.float32)  4.81 us

profile of v4, /device:TPU:119, one launch (start us, length us, event | category | flops | bytes accessed | tf_op | source)
XLA Modules:
  0.0 72.5 jit_solution(8758766883701413765)
XLA Ops:
  0.0 67.7 %shard_map.28 = (bf16[1024,512]{1,0:T(8,128)(2,1)}, bf16[512,1024]{1,0:T(8,128)(2,1)}) custom-call(bf16[1024,256]{1,0:T(8,128)(2,1)} %values_ref.1, s32[4,16]{1,0:T(4,128)} %bitcast.3), custom_call_target="tpu_custom_call" | custom-call | tf_op jit(solution)/shard_map/pallas_call | solution.py:516
  67.7 4.8 %fusion = f32[1024,1024]{1,0:T(8,128)} fusion(bf16[1024,512]{1,0:T(8,128)(2,1)} %get-tuple-element.7, bf16[512,1024]{1,0:T(8,128)(2,1)} %get-tuple-element.8), kind=kOutput, calls=%fused_computation | convolution fusion | flops 1073741824 | bytes 6291456 | tf_op jit(solution)/shard_map/dot_general | solution.py:543
